TPU v7x, 128 devices: a whole 4x4x4 slice. The times are simulated.
128 devices in a mesh: sample: 8 (over y_hi, z), landmark: 16 (over y_lo, x, core).
Axes of the slice: x: 4, y: 4 (y_hi: 2, y_lo: 2; y = y_hi * 2 + y_lo), z: 4, core: 2. Of those that a mesh axis runs over, the one named last changes fastest.
Arguments:
- embeddings: bfloat16 [8192, 4096], P('sample'), may hold values from -6 to 6
- landmarks: bfloat16 [16384, 4096], P('landmark'), may hold values from -6 to 6
- factor: bfloat16 [16384, 16384], P('landmark', 'sample')
- flips: int32 [512, 8192], P(None, 'sample'), may hold values from 0 to 1
- labels: int32 [8192], P('sample'), may hold values from 0 to 1, as said below
- counts: int32 [8], replicated, may hold values from 256 to 1024, as said below
Outputs:
- whitened: bfloat16 [16384, 512], P(('sample', 'landmark'))
- statistic: float32 [512], replicated
Inputs may be any that keep to these rules, and one draw needn't show every extreme that they name: `counts`: one slab holds exactly 1024 live rows. `labels`: 0 or 1; the first slot of every slab is of corpus 0 and the second of corpus 1.
All inputs are finite; a program needn't handle non-finite values.
Results may differ from a plain program's by a relative error of at most 0.029.
Values may be sent and summed in bfloat16 or wider, within the bound.
A program may use at most 128 MiB of HBM per device.

v0:
```python
import math

import jax
import jax.numpy as jnp
from jax import lax
from jax.sharding import PartitionSpec as P

D = 4096
LANDMARKS = 16384


def whiten_maker(factor, moments_half):
    return lax.dot_general(
        factor, moments_half, (((0,), (1,)), ((), ())), preferred_element_type=jnp.float32
    )


def local(embeddings, landmarks, factor, flips, labels, counts):
    slot_count = embeddings.shape[0]
    slab_total = counts.shape[0]
    here_index = lax.axis_index("sample")
    own_count = jnp.sum(jnp.where(jnp.arange(slab_total, dtype=jnp.int32) == here_index, counts, 0))
    live_rows = (jnp.arange(slot_count, dtype=jnp.int32) < own_count).astype(jnp.float32)
    corpus = labels.astype(jnp.float32)
    count_a, count_b = lax.psum(
        (jnp.sum(live_rows * (1.0 - corpus)), jnp.sum(live_rows * corpus)), "sample"
    )
    balance = jnp.sqrt(count_a * count_b / (count_a + count_b))
    row_weight = live_rows * ((1.0 - corpus) / count_a - corpus / count_b) * balance
    wide_x = embeddings.astype(jnp.float32)
    row_scale = lax.rsqrt(jnp.mean(wide_x * wide_x, axis=1) + 1e-06)
    wide_z = landmarks.astype(jnp.float32)
    point_scale = lax.rsqrt(jnp.mean(wide_z * wide_z, axis=1) + 1e-06)
    signs = (2 * flips - 1).astype(jnp.bfloat16)
    cross = lax.dot_general(
        embeddings, landmarks, (((1,), (1,)), ((), ())), preferred_element_type=jnp.float32
    )
    kern = jnp.exp(0.5 * cross * row_scale[:, None] * point_scale[None, :] / math.sqrt(D))
    weighted = (row_weight[:, None] * kern).astype(jnp.bfloat16)
    partial_value = jnp.dot(signs, weighted, preferred_element_type=jnp.float32)
    summed = lax.psum(partial_value.astype(jnp.bfloat16), "sample")
    wide = lax.psum_scatter(
        whiten_maker(factor, summed).astype(jnp.bfloat16),
        "landmark",
        scatter_dimension=0,
        tiled=True,
    ).astype(jnp.float32)
    share = jnp.sum(wide * wide, axis=0)
    statistic = lax.psum(share, ("sample", "landmark")) / LANDMARKS
    return (wide.astype(jnp.bfloat16), statistic)


def solution(mesh):
    return jax.shard_map(
        local,
        mesh=mesh,
        in_specs=(
            P("sample", None),
            P("landmark", None),
            P("landmark", "sample"),
            P(None, "sample"),
            P("sample"),
            P(),
        ),
        out_specs=(P(("sample", "landmark"), None), P()),
        check_vma=False,
    )
```

profile of v0, /device:TPU:1, one launch (start us, length us, event | category | flops | bytes accessed | tf_op | source)
XLA Modules:
  0.0 293.1 jit_solution(10554155324927165992)
XLA Ops:
  7.2 0.0 all-reduce.3.cloned.1.call-start
  7.2 1.3 fusion.9
  8.5 2.0 select_reduce_fusion
  10.5 23.3 %all-reduce = (f32[]{:T(128)}, f32[]{:T(128)}) all-reduce(f32[]{:T(128)} %get-tuple-element.7, f32[]{:T(128)} %get-tuple-element.6), channel_id=1, replica_groups=mesh['sample'=8,'landmark'=16] {'sample'}, use_global_device_ids=true, to_apply=%region_2.3 | all-reduce | flops 2 | bytes 16 | tf_op jit(solution)/shard_map/psum | solution.py:25
  36.3 2.5 select_multiply_fusion
  38.9 0.0 copy-start
  38.9 5.2 %multiply_reduce_fusion.1 = f32[1024]{0:T(1024)S(1)} fusion(bf16[1024,4096]{1,0:T(8,128)(2,1)} %param.6), kind=kLoop, calls=%fused_computation.1 | loop fusion | flops 12581888 | bytes 8392704 | tf_op jit(solution)/shard_map/reduce_sum | solution.py:31
  44.1 0.5 copy-done
  44.7 0.0 copy-start.1
  44.7 1.7 multiply_reduce_fusion
  46.4 0.0 copy-done.1
  46.4 16.2 %fusion.6 = bf16[512,1024]{1,0:T(8,128)(2,1)} fusion(bf16[1024,4096]{1,0:T(8,128)(2,1)} %param.6, bf16[1024,4096]{1,0:T(8,128)(2,1)} %param.7, f32[1024]{0:T(1024)S(1)} %get-tuple-element.10, f32[1024]{0:T(1024)S(1)} %get-tuple-element.11, f32[1024]{0:T(1024)S(1)} %select_multiply_fusion, s32[512,1024]{1,0:T(8,128)S(1)} %copy-done.1), kind=kOutput, calls=%fused_computation.11 | convolution fusion | flops 9671016448 | bytes 19935232 | tf_op jit(solution)/shard_map/dot_general | solution.py:40
  62.6 0.0 all-reduce.3.cloned.1.call-update
  62.6 0.0 reduce-scatter.4.cloned.1.call-start
  62.7 83.6 %all-reduce.3.cloned.1.call-done = bf16[512,1024]{1,0:T(8,128)(2,1)} async-done(((bf16[512,1024]{1,0:T(8,128)(2,1)}), bf16[512,1024]{1,0:T(8,128)(2,1)}) %all-reduce.3.cloned.1.call-update) | async-done | bytes 1048592 | tf_op jit(solution)/shard_map/psum | solution.py:41
  146.3 4.8 %fusion = bf16[2048,512]{0,1:T(8,128)(2,1)S(1)} fusion(bf16[512,1024]{1,0:T(8,128)(2,1)} %all-reduce.3.cloned.1.call-done, bf16[1024,2048]{1,0:T(8,128)(2,1)} %param.8), kind=kOutput, calls=%fused_computation.4 | convolution fusion | flops 2148532224 | bytes 7340032 | tf_op jit(solution)/shard_map/dot_general | solution.py:13
  151.1 2.5 copy.10
  153.6 0.0 reduce-scatter.4.cloned.1.call-update
  153.7 62.8 %reduce-scatter.4.cloned.1.call-done = bf16[128,512]{1,0:T(8,128)(2,1)} async-done(((bf16[2048,512]{1,0:T(8,128)(2,1)}), bf16[128,512]{1,0:T(8,128)(2,1)}) %reduce-scatter.4.cloned.1.call-update) | async-done | bytes 131088
  216.4 1.0 copy.11
  217.4 0.2 multiply_reduce_fusion.2
  217.6 68.1 %psum.31 = f32[512]{0:T(512)S(1)} all-reduce(f32[512]{0:T(512)S(1)} %multiply_reduce_fusion.2), channel_id=1, replica_groups=mesh['sample'=8,'landmark'=16] {'sample','landmark'}, use_global_device_ids=true, to_apply=%region_10.11 | all-reduce | flops 512 | bytes 4096 | tf_op jit(solution)/shard_map/psum | solution.py:49
  285.7 0.6 broadcast_multiply_fusion
  (1 shorter events, 0.0 us)
Async XLA Ops:
  7.2 139.1 %all-reduce.3.cloned.1.call-start = ((), (), s32[]{:S(2)}) async-start(), calls=%async_computation.1 | async-start | bytes 2097152 | tf_op jit(solution)/shard_map/psum | solution.py:41
  38.9 5.8 %copy-start = (bf16[1024,4096]{1,0:T(8,128)(2,1)S(1)}, bf16[1024,4096]{1,0:T(8,128)(2,1)}, u32[]{:S(2)}) copy-start(bf16[1024,4096]{1,0:T(8,128)(2,1)} %param.7) | copy-start | bytes 25165828
  44.7 1.7 copy-start.1
  62.6 153.8 %reduce-scatter.4.cloned.1.call-start = ((), (), s32[]{:S(2)}) async-start(), calls=%async_computation.2 | async-start | bytes 2228224
Sparse Core Ops, SparseCore 0:
  62.7 83.4 all-reduce.2
  153.8 62.5 reduce-scatter.3
where the time goes:
time: 293 us
  waiting for transfers between devices  146 us (50%)
  blocking collectives  91.4 us (31%)
  matrix products  21.1 us (7%)
  between operations  16.6 us (6%)
  other arithmetic  13.5 us (5%)
  local copies, waits for them, and re-layouts  4.09 us (1%)
    psum x1, waiting for transfers between devices, local(): summed = lax.psum(partial_value.astype(jnp.bfloat16), 'sample')  83.6 us
    psum x1, blocking collectives, local(): statistic = lax.psum(share, ('sample', 'landmark')) / LANDMARKS  68.1 us
    unnamed x3, waiting for transfers between devices  62.8 us
    psum x1, blocking collectives, local(): lax.psum((jnp.sum(live_rows * (1.0 - corpus)), jnp.sum(live_rows * corpus...  23.3 us
    dot_general x1, matrix products, local(): partial_value = jnp.dot(signs, weighted, preferred_element_type=jnp.float32)  16.2 us
  transfers between devices with their start and end apart: 2, of which 2 were waited for; matrix products, arithmetic and copies ran while one was open for 0% of the time, Pallas kernels for 0%

commit v1 on v0

v1 whole, which is shorter than its diff:
```python
import jax
import jax.numpy as jnp
from jax import lax
from jax.experimental import pallas as pl
from jax.experimental.pallas import tpu as pltpu
from jax.sharding import PartitionSpec as P

D = 4096
LANDMARKS = 16384
MESH = pl.DeviceIdType.MESH
F32 = jnp.float32
BF16 = jnp.bfloat16
CHUNK = 256
CHUNKS = 4
ROWS = 1024
BLOCK = 256
BLOCKS = ROWS // BLOCK
HALF = 32

SLABS = [(1, 2), (1, 1), (1, 3), (0, 2), (1, 0), (0, 1), (0, 3)]
CHIPS = [(1, 2), (1, 1), (1, 3), (0, 2), (1, 0), (0, 1), (0, 3)]


def kernel(
    counts_ref, labels_ref, emb_hbm, land_hbm, factor_hbm, flips_hbm,
    white_ref, stat_ref,
    emb, land, factor, flips, signs, weighted, row_scale, col_a, col_b, col_w,
    partial_buf, slab_in, own_sum, moments, acc, wide_out, wide_in, wide_rows,
    count_out, count_in, stat_out, stat_in, total_out, total_in,
    emb_sem, land_sem, factor_sem, flips_sem,
    factor_send, factor_recv, count_send, count_recv, slab_send, slab_recv,
    mom_send, mom_recv, wide_send, wide_recv, stat_send, stat_recv, total_send, total_recv,
):
    slab = lax.axis_index("sample")
    place = lax.axis_index("landmark")
    y_hi, z = slab // 4, slab % 4
    y_lo, x, core = place // 8, (place // 2) % 4, place % 2
    other = (core + 1) % 2

    def slab_at(offset):
        return ((y_hi + offset[0]) % 2) * 4 + (z + offset[1]) % 4

    def chip_at(offset):
        return ((y_lo + offset[0]) % 2) * 4 + (x + offset[1]) % 4

    def core_at(step):
        return (core + step) % 2

    here = (y_lo * 4 + x) * 2

    def emb_copy(b):
        rows = pl.ds(b * BLOCK, BLOCK)
        return pltpu.make_async_copy(emb_hbm.at[rows], emb.at[rows], emb_sem.at[b])

    def land_copy(k):
        rows = pl.ds(k * CHUNK, CHUNK)
        return pltpu.make_async_copy(land_hbm.at[rows], land.at[rows], land_sem.at[k])

    def factor_copy(k):
        return pltpu.make_async_copy(
            factor_hbm.at[pl.ds(k * CHUNK, CHUNK)],
            factor.at[k, pl.ds(core * CHUNK, CHUNK)],
            factor_sem.at[k],
        )

    def factor_share(k):
        return pltpu.make_async_remote_copy(
            src_ref=factor_hbm.at[pl.ds(k * CHUNK, CHUNK)],
            dst_ref=factor.at[k, pl.ds(core * CHUNK, CHUNK)],
            send_sem=factor_send.at[k],
            recv_sem=factor_recv.at[k],
            device_id=(slab, here + other),
            device_id_type=MESH,
        )

    flips_copy = pltpu.make_async_copy(flips_hbm, flips, flips_sem)
    land_copy(0).start()
    for b in range(BLOCKS):
        emb_copy(b).start()
    flips_copy.start()
    for k in range(1, CHUNKS):
        land_copy(k).start()

    barrier = pltpu.get_barrier_semaphore()
    friends = [(slab, here + other)]
    for offset in SLABS:
        for step in range(2):
            friends.append((slab_at(offset), here + core_at(step)))
    for offset in CHIPS:
        for step in range(2):
            friends.append((slab, chip_at(offset) * 2 + core_at(step)))
    for friend in friends:
        pl.semaphore_signal(barrier, inc=1, device_id=friend, device_id_type=MESH)

    own_count = counts_ref[slab]
    corpus = labels_ref[...].astype(F32)
    slot = lax.broadcasted_iota(jnp.int32, (8, 128), 0) * 128 + lax.broadcasted_iota(
        jnp.int32, (8, 128), 1
    )
    live = jnp.where(slot < own_count, 1.0, 0.0).astype(F32)
    in_a, in_b = live * (1.0 - corpus), live * corpus
    count_out[0] = jnp.broadcast_to(jnp.sum(in_a, keepdims=True), (8, 128))
    count_out[1] = jnp.broadcast_to(jnp.sum(in_b, keepdims=True), (8, 128))

    pl.semaphore_wait(barrier, len(friends))

    def count_copy(i):
        return pltpu.make_async_remote_copy(
            src_ref=count_out,
            dst_ref=count_in.at[i],
            send_sem=count_send.at[i],
            recv_sem=count_recv.at[i],
            device_id=(slab_at(SLABS[i]), place),
            device_id_type=MESH,
        )

    for i in range(7):
        count_copy(i).start()
    for k in range(CHUNKS):
        factor_copy(k).start()
        factor_share(k).start()

    for i in range(8):
        rows = pl.ds(i * 128, 128)
        col_a[rows, :] = jnp.transpose(jnp.broadcast_to(in_a[i : i + 1], (128, 128)))
        col_b[rows, :] = jnp.transpose(jnp.broadcast_to(in_b[i : i + 1], (128, 128)))

    def squares(ref, start, count):
        total = jnp.zeros((count, 128), F32)
        for t in range(D // 128):
            value = ref[pl.ds(start, count), pl.ds(t * 128, 128)].astype(F32)
            total = total + value * value
        return total

    def point_scale(k):
        parts = []
        for q in range(CHUNK // 128):
            total = squares(land, pl.multiple_of(k * CHUNK + q * 128, 128), 128)
            parts.append(jnp.sum(jnp.transpose(total), axis=0, keepdims=True))
        return lax.rsqrt(jnp.concatenate(parts, axis=1) * (1.0 / D) + 1e-6)

    def wide2(value):
        return jnp.concatenate([value, value], axis=1)

    fold = 0.5 / 64.0 * 1.4426950408889634

    def slab_copy(k, i):
        there = slab_at(SLABS[i])
        return pltpu.make_async_remote_copy(
            src_ref=partial_buf.at[k, pl.ds(there * 64, 64)],
            dst_ref=slab_in.at[k, i],
            send_sem=slab_send.at[k, i],
            recv_sem=slab_recv.at[k, i],
            device_id=(there, place),
            device_id_type=MESH,
        )

    def send_moments(k):
        partial_buf[k] = jnp.dot(
            signs[...], weighted[...], preferred_element_type=F32
        ).astype(BF16)
        for i in range(7):
            slab_copy(k, i).start()

    def mom_copy(k, n):
        if n < 14:
            there, step = slab_at(SLABS[n // 2]), n % 2
        else:
            there, step = slab, 1
        return pltpu.make_async_remote_copy(
            src_ref=own_sum.at[k, pl.ds(core_at(step) * HALF, HALF)],
            dst_ref=moments.at[k, core, pl.ds(slab * HALF, HALF)],
            send_sem=mom_send.at[k, n],
            recv_sem=mom_recv.at[k, n],
            device_id=(there, here + core_at(step)),
            device_id_type=MESH,
        )

    def sum_slabs(k):
        total = partial_buf[k, pl.ds(slab * 64, 64), :].astype(F32)
        for i in range(7):
            slab_copy(k, i).wait_recv()
        for i in range(7):
            total = total + slab_in[k, i].astype(F32)
        own_sum[k] = total.astype(BF16)
        for n in range(15):
            mom_copy(k, n).start()
        moments[k, core, pl.ds(slab * HALF, HALF), :] = own_sum[
            k, pl.ds(core * HALF, HALF), :
        ]

    land_copy(0).wait()
    first_scale = point_scale(0)

    def first_block(b, _):
        start = pl.multiple_of(b * BLOCK, BLOCK)
        emb_copy(b).wait()
        for q in range(BLOCK // 64):
            rows = pl.multiple_of(start + q * 64, 64)
            total = jnp.sum(squares(emb, rows, 64), axis=1, keepdims=True)
            row_scale[pl.ds(rows, 64), :] = jnp.broadcast_to(
                lax.rsqrt(total * (1.0 / D) + 1e-6) * fold, (64, 128)
            )
        cross = lax.dot_general(
            emb[pl.ds(start, BLOCK), :],
            land[0:CHUNK, :],
            (((1,), (1,)), ((), ())),
            preferred_element_type=F32,
        )
        scale = wide2(row_scale[pl.ds(start, BLOCK), :])

        @pl.when(b == 0)
        def _():
            for i in range(7):
                count_copy(i).wait()
            count_a, count_b = count_out[0], count_out[1]
            for i in range(7):
                count_a = count_a + count_in[i, 0]
                count_b = count_b + count_in[i, 1]
            balance = jnp.sqrt(count_a * count_b / (count_a + count_b))
            gain_a = (balance / count_a)[0:1]
            gain_b = (balance / count_b)[0:1]
            col_w[...] = col_a[...] * gain_a - col_b[...] * gain_b

        weight = wide2(col_w[pl.ds(start, BLOCK), :])
        weighted[pl.ds(start, BLOCK), :] = (
            jnp.exp2(cross * scale * first_scale) * weight
        ).astype(BF16)
        return 0

    lax.fori_loop(0, BLOCKS, first_block, 0)
    flips_copy.wait()
    signs[...] = (2 * flips[...] - 1).astype(F32).astype(BF16)
    send_moments(0)

    def later_chunk(k, _):
        land_copy(k).wait()
        points = point_scale(k)
        cross = lax.dot_general(
            emb[...],
            land[pl.ds(pl.multiple_of(k * CHUNK, CHUNK), CHUNK), :],
            (((1,), (1,)), ((), ())),
            preferred_element_type=F32,
        )
        weighted[...] = (
            jnp.exp2(cross * wide2(row_scale[...]) * points) * wide2(col_w[...])
        ).astype(BF16)
        send_moments(k)

        @pl.when(k >= 2)
        def _():
            sum_slabs(k - 2)

        return 0

    lax.fori_loop(1, CHUNKS, later_chunk, 0)

    def moments_of(k):
        for n in range(15):
            mom_copy(k, n).wait_recv()
        return jnp.concatenate([moments[k, 0], moments[k, 1]], axis=1)

    def whiten(k):
        left = moments_of(k)

        def tile(q, _):
            value = jnp.dot(
                left,
                factor[k, :, pl.ds(pl.multiple_of(q * 256, 256), 256)],
                preferred_element_type=F32,
            )
            if k == 0:
                acc[q] = value
            else:
                acc[q] = acc[q] + value
            return 0

        lax.fori_loop(0, 8, tile, 0)

    sum_slabs(CHUNKS - 2)
    for k in range(CHUNKS):
        factor_copy(k).wait()
        factor_share(k).wait()
    whiten(0)
    sum_slabs(CHUNKS - 1)
    for k in range(1, CHUNKS - 1):
        whiten(k)

    def wide_copy(t, step):
        chip = chip_at(CHIPS[t]) if t < 7 else y_lo * 4 + x
        return pltpu.make_async_remote_copy(
            src_ref=wide_out.at[t, core_at(step)],
            dst_ref=wide_in.at[t, core],
            send_sem=wide_send.at[t, step],
            recv_sem=wide_recv.at[t, step],
            device_id=(slab, chip * 2 + core_at(step)),
            device_id_type=MESH,
        )

    last = CHUNKS - 1
    left = moments_of(last)
    for t in range(8):
        q = chip_at(CHIPS[t]) if t < 7 else y_lo * 4 + x
        value = acc[q] + jnp.dot(
            left,
            factor[last, :, pl.ds(pl.multiple_of(q * 256, 256), 256)],
            preferred_element_type=F32,
        )
        value = value.astype(BF16)
        wide_out[t, 0] = value[:, :128]
        wide_out[t, 1] = value[:, 128:]
        if t < 7:
            wide_copy(t, 0).start()
        wide_copy(t, 1).start()
    wide_in[7, core] = wide_out[7, core]

    for t in range(8):
        if t < 7:
            wide_copy(t, 0).wait_recv()
        wide_copy(t, 1).wait_recv()
    for c in range(2):
        total = wide_in[0, c].astype(F32)
        for t in range(1, 8):
            total = total + wide_in[t, c].astype(F32)
        for s in range(8):
            wide_rows[pl.ds(s * 64 + c * HALF, HALF), :] = total[s * HALF : (s + 1) * HALF]
    stat_out[...] = jnp.zeros((8, 128), F32)
    for i in range(4):
        turned = jnp.transpose(wide_rows[pl.ds(i * 128, 128), :])
        white_ref[:, pl.ds(i * 128, 128)] = turned.astype(BF16)
        stat_out[pl.ds(i, 1), :] = jnp.sum(turned * turned, axis=0, keepdims=True)

    def stat_copy(n):
        if n < 14:
            there, step = chip_at(CHIPS[n // 2]), n % 2
        else:
            there, step = y_lo * 4 + x, 1
        return pltpu.make_async_remote_copy(
            src_ref=stat_out,
            dst_ref=stat_in.at[place],
            send_sem=stat_send.at[n],
            recv_sem=stat_recv.at[n],
            device_id=(slab, there * 2 + core_at(step)),
            device_id_type=MESH,
        )

    for n in range(15):
        stat_copy(n).start()
    stat_in[place] = stat_out[...]
    for n in range(15):
        stat_copy(n).wait_recv()
    total = stat_in[0]
    for n in range(1, 16):
        total = total + stat_in[n]
    total_out[...] = total

    def total_copy(i):
        return pltpu.make_async_remote_copy(
            src_ref=total_out,
            dst_ref=total_in.at[slab],
            send_sem=total_send.at[i],
            recv_sem=total_recv.at[i],
            device_id=(slab_at(SLABS[i]), place),
            device_id_type=MESH,
        )

    for i in range(7):
        total_copy(i).start()
    total_in[slab] = total_out[...]

    for k in range(CHUNKS):
        for i in range(7):
            slab_copy(k, i).wait_send()
        for n in range(15):
            mom_copy(k, n).wait_send()
    for t in range(8):
        if t < 7:
            wide_copy(t, 0).wait_send()
        wide_copy(t, 1).wait_send()
    for n in range(15):
        stat_copy(n).wait_send()

    for i in range(7):
        total_copy(i).wait()
    total = total_in[0]
    for i in range(1, 8):
        total = total + total_in[i]
    stat_ref[...] = total[0:4] * (1.0 / LANDMARKS)


def local(embeddings, landmarks, factor, flips, labels, counts):
    any_space = pl.BlockSpec(memory_space=pl.ANY)
    vmem = pl.BlockSpec(memory_space=pltpu.VMEM)
    dma = pltpu.SemaphoreType.DMA
    whitened, statistic = pl.pallas_call(
        kernel,
        out_shape=(
            jax.ShapeDtypeStruct((128, 512), BF16),
            jax.ShapeDtypeStruct((4, 128), F32),
        ),
        in_specs=[pl.BlockSpec(memory_space=pltpu.SMEM), vmem] + [any_space] * 4,
        out_specs=(vmem, vmem),
        scratch_shapes=[
            pltpu.VMEM((ROWS, D), BF16),
            pltpu.VMEM((CHUNK * CHUNKS, D), BF16),
            pltpu.VMEM((CHUNKS, 2 * CHUNK, 2048), BF16),
            pltpu.VMEM((512, ROWS), jnp.int32),
            pltpu.VMEM((512, ROWS), BF16),
            pltpu.VMEM((ROWS, CHUNK), BF16),
            pltpu.VMEM((ROWS, 128), F32),
            pltpu.VMEM((ROWS, 128), F32),
            pltpu.VMEM((ROWS, 128), F32),
            pltpu.VMEM((ROWS, 128), F32),
            pltpu.VMEM((CHUNKS, 512, CHUNK), BF16),
            pltpu.VMEM((CHUNKS, 7, 64, CHUNK), BF16),
            pltpu.VMEM((CHUNKS, 64, CHUNK), BF16),
            pltpu.VMEM((CHUNKS, 2, 256, CHUNK), BF16),
            pltpu.VMEM((8, 256, 256), F32),
            pltpu.VMEM((8, 2, 256, 128), BF16),
            pltpu.VMEM((8, 2, 256, 128), BF16),
            pltpu.VMEM((512, 128), F32),
            pltpu.VMEM((2, 8, 128), F32),
            pltpu.VMEM((7, 2, 8, 128), F32),
            pltpu.VMEM((8, 128), F32),
            pltpu.VMEM((16, 8, 128), F32),
            pltpu.VMEM((8, 128), F32),
            pltpu.VMEM((8, 8, 128), F32),
            dma((BLOCKS,)),
            dma((CHUNKS,)),
            dma((CHUNKS,)),
            dma,
            dma((CHUNKS,)),
            dma((CHUNKS,)),
            dma((7,)),
            dma((7,)),
            dma((CHUNKS, 7)),
            dma((CHUNKS, 7)),
            dma((CHUNKS, 15)),
            dma((CHUNKS, 15)),
            dma((8, 2)),
            dma((8, 2)),
            dma((15,)),
            dma((15,)),
            dma((7,)),
            dma((7,)),
        ],
        compiler_params=pltpu.CompilerParams(
            collective_id=0, has_side_effects=True, vmem_limit_bytes=60 << 20
        ),
    )(counts, labels.reshape(8, 128), embeddings, landmarks, factor, flips)
    return whitened, statistic.reshape(512)


def solution(mesh):
    return jax.shard_map(
        local,
        mesh=mesh,
        in_specs=(
            P("sample", None),
            P("landmark", None),
            P("landmark", "sample"),
            P(None, "sample"),
            P("sample"),
            P(),
        ),
        out_specs=(P(("sample", "landmark"), None), P()),
        check_vma=False,
    )
```

time: 293 us -> 74.4 us (0.25)
  waiting for transfers between devices: 146 us -> 0 us
  blocking collectives: 91.4 us -> 0 us
  Pallas kernels: 0 us -> 70.7 us
  matrix products: 21.1 us -> 0 us
  between operations: 16.6 us -> 0.64 us
  other arithmetic: 13.5 us -> 0 us
    psum x2 -> x0, blocking collectives: 91.4 us -> none  [the longest x1 68.1 us: local(): statistic = lax.psum(share, ('sample', 'landmark')) / LANDMARKS]
    psum x1 -> x0, waiting for transfers between devices: 83.6 us -> none  [local(): summed = lax.psum(partial_value.astype(jnp.bfloat16), 'sample')]
    pallas_call x0 -> x1, Pallas kernels: none -> 70.7 us  [local(): pl.pallas_call(kernel, out_shape=(jax.ShapeDtypeStruct((128, 512), BF16),...]
    unnamed x3 -> x0, waiting for transfers between devices: 62.8 us -> none
    dot_general x2 -> x0, matrix products: 21.1 us -> none  [the longest x1 16.2 us: local(): partial_value = jnp.dot(signs, weighted, preferred_element_type=jnp.float32)]
    reduce_sum x5 -> x0, other arithmetic: 10.4 us -> none  [the longest x1 5.22 us: local(): row_scale = lax.rsqrt(jnp.mean(wide_x * wide_x, axis=1) + 1e-06)]
  transfers between devices with their start and end apart: 2 -> 0, of which waited for: 2 -> 0; matrix products, arithmetic and copies ran while one was open for 0% -> 0% of each run, Pallas kernels for 0% -> 0%
where the time goes in v1:
time: 74.4 us; the launch traced here: 74.2 us
  Pallas kernels  70.7 us (95%)
  local copies, waits for them, and re-layouts  2.83 us (4%)
    pallas_call x1, Pallas kernels, local(): pl.pallas_call(kernel, out_shape=(jax.ShapeDtypeStruct((128, 512), BF16),...  70.7 us
    unnamed x2, local copies, waits for them, and re-layouts  2.83 us

profile of v1, /device:TPU:1, one launch (start us, length us, event | category | flops | bytes accessed | tf_op | source)
XLA Modules:
  0.0 74.2 jit_solution(31556649831731777)
XLA Ops:
  0.6 70.7 %shard_map.77 = (bf16[128,512]{1,0:T(8,128)(2,1)}, f32[4,128]{1,0:T(4,128)}) custom-call(s32[8]{0:T(128)} %counts_ref.1, s32[8,128]{1,0:T(8,128)} %bitcast.2, bf16[1024,4096]{1,0:T(8,128)(2,1)} %emb_hbm.1, bf16[1024,4096]{1,0:T(8,128)(2,1)} %land_hbm.1, bf16[1024,2048]{1,0:T(8,128)(2,1)} %factor_hbm.1, s32[512,1024]{1,0:T(8,128)} %flips_hbm.1), custom_call_target="tpu_custom_call" | custom-call | tf_op jit(solution)/shard_map/pallas_call | solution.py:395
  71.4 1.6 %copy.10 = bf16[128,512]{1,0:T(8,128)(2,1)} copy(bf16[128,512]{1,0:T(8,128)(2,1)} %get-tuple-element.8) | data formatting | bytes 262144
  72.9 1.3 %copy.11 = f32[512]{0:T(512)} copy(f32[512]{0:T(512)} %bitcast.3) | data formatting | bytes 4096

commit v2 on v1

v2 whole, which is shorter than its diff:
```python
import jax
import jax.numpy as jnp
from jax import lax
from jax.experimental import pallas as pl
from jax.experimental.pallas import tpu as pltpu
from jax.sharding import PartitionSpec as P

D = 4096
LANDMARKS = 16384
MESH = pl.DeviceIdType.MESH
F32 = jnp.float32
BF16 = jnp.bfloat16
CHUNK = 256
CHUNKS = 4
ROWS = 1024
BLOCK = 256
BLOCKS = ROWS // BLOCK
PART = 16

SLABS = [(1, 2), (1, 1), (1, 3), (0, 2), (1, 0), (0, 1), (0, 3)]
CHIPS = [(1, 2), (1, 1), (1, 3), (0, 2), (1, 0), (0, 1), (0, 3)]


def kernel(
    counts_ref, labels_ref, emb_hbm, land_hbm, factor_hbm, flips_hbm,
    white_ref, stat_ref,
    emb, land, factor, flips, signs, weighted, row_scale, col_a, col_b, col_w, kern,
    partial_buf, slab_in, own_sum, moments, wide_out, wide_in, wide_rows,
    count_out, count_in, stat_out, stat_in, total_out, total_in,
    emb_sem, land_sem, factor_sem, flips_sem,
    factor_send, factor_recv, count_send, count_recv, slab_send, slab_recv,
    early_send, early_recv, late_send, late_recv, wide_send, wide_recv, stat_send, stat_recv, total_send, total_recv,
):
    slab = lax.axis_index("sample")
    place = lax.axis_index("landmark")
    y_hi, z = slab // 4, slab % 4
    y_lo, x, core = place // 8, (place // 2) % 4, place % 2
    other = (core + 1) % 2

    def slab_at(offset):
        return ((y_hi + offset[0]) % 2) * 4 + (z + offset[1]) % 4

    def chip_at(offset):
        return ((y_lo + offset[0]) % 2) * 4 + (x + offset[1]) % 4

    def core_at(step):
        return (core + step) % 2

    here = (y_lo * 4 + x) * 2

    def settle(like, sem):
        pltpu.make_async_copy(like, like, sem).wait()

    def emb_copy(b):
        rows = pl.ds(b * BLOCK, BLOCK)
        return pltpu.make_async_copy(emb_hbm.at[rows], emb.at[rows], emb_sem.at[b])

    def land_copy(k):
        rows = pl.ds(k * CHUNK, CHUNK)
        return pltpu.make_async_copy(land_hbm.at[rows], land.at[rows], land_sem.at[k])

    def factor_copy(k):
        return pltpu.make_async_copy(
            factor_hbm.at[pl.ds(k * CHUNK, CHUNK)],
            factor.at[core, pl.ds(k * CHUNK, CHUNK)],
            factor_sem,
        )

    def factor_share(k):
        return pltpu.make_async_remote_copy(
            src_ref=factor_hbm.at[pl.ds(k * CHUNK, CHUNK)],
            dst_ref=factor.at[core, pl.ds(k * CHUNK, CHUNK)],
            send_sem=factor_send,
            recv_sem=factor_recv,
            device_id=(slab, here + other),
            device_id_type=MESH,
        )

    flips_copy = pltpu.make_async_copy(flips_hbm, flips, flips_sem)
    land_copy(0).start()
    for b in range(BLOCKS):
        emb_copy(b).start()

    barrier = pltpu.get_barrier_semaphore()
    friends = [(slab, here + other)]
    for offset in SLABS:
        for step in range(2):
            friends.append((slab_at(offset), here + core_at(step)))
    for offset in CHIPS:
        for step in range(2):
            friends.append((slab, chip_at(offset) * 2 + core_at(step)))
    for friend in friends:
        pl.semaphore_signal(barrier, inc=1, device_id=friend, device_id_type=MESH)

    own_count = counts_ref[slab]
    corpus = labels_ref[...].astype(F32)
    slot = lax.broadcasted_iota(jnp.int32, (8, 128), 0) * 128 + lax.broadcasted_iota(
        jnp.int32, (8, 128), 1
    )
    live = jnp.where(slot < own_count, 1.0, 0.0).astype(F32)
    in_a, in_b = live * (1.0 - corpus), live * corpus
    count_out[0] = jnp.broadcast_to(jnp.sum(in_a, keepdims=True), (8, 128))
    count_out[1] = jnp.broadcast_to(jnp.sum(in_b, keepdims=True), (8, 128))

    def squares(ref, start, count):
        total = jnp.zeros((count, 128), F32)
        for t in range(D // 128):
            value = ref[pl.ds(start, count), pl.ds(t * 128, 128)].astype(F32)
            total = total + value * value
        return total

    def lane_sums(value):
        return lax.dot_general(
            jnp.ones((8, 128), F32),
            value,
            (((1,), (1,)), ((), ())),
            precision=lax.Precision.HIGHEST,
            preferred_element_type=F32,
        )

    def point_scale(k):
        parts = []
        for q in range(CHUNK // 64):
            parts.append(squares(land, pl.multiple_of(k * CHUNK + q * 64, 64), 64))
        total = lane_sums(jnp.concatenate(parts, axis=0))
        return lax.rsqrt(total[0:1] * (1.0 / D) + 1e-6)

    def wide2(value):
        return jnp.concatenate([value, value], axis=1)

    fold = 0.5 / 64.0 * 1.4426950408889634

    def slab_copy(k, i):
        there = slab_at(SLABS[i])
        return pltpu.make_async_remote_copy(
            src_ref=partial_buf.at[k, pl.ds(there * 64, 64)],
            dst_ref=slab_in.at[k, i],
            send_sem=slab_send,
            recv_sem=slab_recv.at[k],
            device_id=(there, place),
            device_id_type=MESH,
        )

    def send_moments(k):
        partial_buf[k] = jnp.dot(
            signs[...], weighted[...], preferred_element_type=F32
        ).astype(BF16)
        for i in range(7):
            slab_copy(k, i).start()

    def mom_target(n):
        if n < 14:
            return slab_at(SLABS[n // 2]), n % 2
        return slab, 1

    def early_copy(k, n):
        there, step = mom_target(n)
        columns = pl.ds(k * CHUNK, CHUNK)
        return pltpu.make_async_remote_copy(
            src_ref=own_sum.at[0, core_at(step), :, columns],
            dst_ref=moments.at[0, core * 8 + slab, :, columns],
            send_sem=early_send,
            recv_sem=early_recv,
            device_id=(there, here + core_at(step)),
            device_id_type=MESH,
        )

    def late_copy(n):
        there, step = mom_target(n)
        return pltpu.make_async_remote_copy(
            src_ref=own_sum.at[1, core_at(step)],
            dst_ref=moments.at[1, core * 8 + slab],
            send_sem=late_send,
            recv_sem=late_recv,
            device_id=(there, here + core_at(step)),
            device_id_type=MESH,
        )

    def sum_slabs(k):
        total = partial_buf[k, pl.ds(slab * 64, 64), :].astype(F32)
        settle(slab_in.at[k], slab_recv.at[k])
        for i in range(7):
            total = total + slab_in[k, i].astype(F32)
        total = total.astype(BF16)
        columns = pl.ds(pl.multiple_of(k * CHUNK, CHUNK), CHUNK)
        for c in range(2):
            for h in range(2):
                start = (2 * c + h) * PART
                own_sum[h, c, :, columns] = total[start : start + PART]
        for n in range(15):
            early_copy(k, n).start()

    land_copy(0).wait()
    first_scale = point_scale(0)

    def first_block(b, _):
        start = pl.multiple_of(b * BLOCK, BLOCK)
        emb_copy(b).wait()
        for q in range(BLOCK // 64):
            rows = pl.multiple_of(start + q * 64, 64)
            total = jnp.sum(squares(emb, rows, 64), axis=1, keepdims=True)
            row_scale[pl.ds(rows, 64), :] = jnp.broadcast_to(
                lax.rsqrt(total * (1.0 / D) + 1e-6) * fold, (64, 128)
            )
        cross = lax.dot_general(
            emb[pl.ds(start, BLOCK), :],
            land[0:CHUNK, :],
            (((1,), (1,)), ((), ())),
            preferred_element_type=F32,
        )
        scale = wide2(row_scale[pl.ds(start, BLOCK), :])
        kern[pl.ds(start, BLOCK), :] = jnp.exp2(cross * scale * first_scale)
        return 0

    first_block(0, 0)
    pl.semaphore_wait(barrier, len(friends))

    def count_copy(i):
        return pltpu.make_async_remote_copy(
            src_ref=count_out,
            dst_ref=count_in.at[i],
            send_sem=count_send,
            recv_sem=count_recv,
            device_id=(slab_at(SLABS[i]), place),
            device_id_type=MESH,
        )

    for i in range(7):
        count_copy(i).start()
    flips_copy.start()
    for k in range(1, CHUNKS):
        land_copy(k).start()
    lax.fori_loop(1, BLOCKS, first_block, 0)

    eye = lax.broadcasted_iota(jnp.int32, (128, 128), 0) == lax.broadcasted_iota(
        jnp.int32, (128, 128), 1
    )
    for row, column in ((in_a, col_a), (in_b, col_b)):
        for i in range(8):
            spread = jnp.where(eye, jnp.broadcast_to(row[i : i + 1], (128, 128)), 0.0)
            column[pl.ds(i * 128, 128), :] = jnp.dot(
                spread.astype(BF16), jnp.ones((128, 128), BF16), preferred_element_type=F32
            )
    flips_copy.wait()
    signs[...] = (2 * flips[...] - 1).astype(F32).astype(BF16)
    settle(count_in, count_send)
    settle(count_in, count_recv)
    count_a, count_b = count_out[0], count_out[1]
    for i in range(7):
        count_a = count_a + count_in[i, 0]
        count_b = count_b + count_in[i, 1]
    balance = jnp.sqrt(count_a * count_b / (count_a + count_b))
    gain_a = (balance / count_a)[0:1]
    gain_b = (balance / count_b)[0:1]
    col_w[...] = col_a[...] * gain_a - col_b[...] * gain_b
    weighted[...] = (kern[...] * wide2(col_w[...])).astype(BF16)
    send_moments(0)
    for k in range(CHUNKS):
        factor_copy(k).start()
        factor_share(k).start()

    def later_chunk(k, _):
        land_copy(k).wait()
        points = point_scale(k)
        cross = lax.dot_general(
            emb[...],
            land[pl.ds(pl.multiple_of(k * CHUNK, CHUNK), CHUNK), :],
            (((1,), (1,)), ((), ())),
            preferred_element_type=F32,
        )
        weighted[...] = (
            jnp.exp2(cross * wide2(row_scale[...]) * points) * wide2(col_w[...])
        ).astype(BF16)
        send_moments(k)

        @pl.when(k >= 2)
        def _():
            sum_slabs(k - 2)

        return 0

    lax.fori_loop(1, CHUNKS, later_chunk, 0)

    sum_slabs(CHUNKS - 2)
    sum_slabs(CHUNKS - 1)
    for n in range(15):
        late_copy(n).start()
    for h in range(2):
        moments[h, core * 8 + slab] = own_sum[h, core]
    settle(factor.at[core], factor_sem)
    settle(factor.at[core], factor_send)
    settle(factor.at[other], factor_recv)

    def wide_copy(h, t, step):
        chip = chip_at(CHIPS[t]) if t < 7 else y_lo * 4 + x
        return pltpu.make_async_remote_copy(
            src_ref=wide_out.at[h, t, core_at(step)],
            dst_ref=wide_in.at[h, core * 8 + t],
            send_sem=wide_send,
            recv_sem=wide_recv.at[h],
            device_id=(slab, chip * 2 + core_at(step)),
            device_id_type=MESH,
        )

    def whiten(h):
        left = jnp.concatenate(
            [moments[h, c * 8 : c * 8 + 8].reshape(8 * PART, ROWS) for c in range(2)], axis=1
        )
        for t in range(8):
            q = chip_at(CHIPS[t]) if t < 7 else y_lo * 4 + x
            columns = pl.ds(pl.multiple_of(q * 256, 256), 256)
            value = jnp.dot(
                left,
                jnp.concatenate([factor[0, :, columns], factor[1, :, columns]], axis=0),
                preferred_element_type=F32,
            ).astype(BF16)
            wide_out[h, t, 0] = value[:, :128]
            wide_out[h, t, 1] = value[:, 128:]
            if t < 7:
                wide_copy(h, t, 0).start()
            wide_copy(h, t, 1).start()
        wide_in[h, core * 8 + 7] = wide_out[h, 7, core]

    def gather(h):
        settle(wide_in.at[h, pl.ds(0, 15)], wide_recv.at[h])
        for c in range(2):
            total = wide_in[h, c * 8].astype(F32)
            for t in range(1, 8):
                total = total + wide_in[h, c * 8 + t].astype(F32)
            for s in range(8):
                wide_rows[pl.ds(s * 64 + c * 32 + h * PART, PART), :] = total[
                    s * PART : (s + 1) * PART
                ]

    settle(moments.at[0, pl.ds(0, 15)], early_recv)
    whiten(0)
    settle(moments.at[1, pl.ds(0, 15)], late_recv)
    whiten(1)
    gather(0)
    gather(1)
    values = wide_rows[...]
    norms = lane_sums(values * values)[0:1]
    for i in range(4):
        stat_out[pl.ds(i, 1), :] = norms[:, i * 128 : (i + 1) * 128]
    stat_out[pl.ds(4, 4), :] = jnp.zeros((4, 128), F32)

    def stat_copy(n):
        if n < 14:
            there, step = chip_at(CHIPS[n // 2]), n % 2
        else:
            there, step = y_lo * 4 + x, 1
        return pltpu.make_async_remote_copy(
            src_ref=stat_out,
            dst_ref=stat_in.at[place],
            send_sem=stat_send,
            recv_sem=stat_recv,
            device_id=(slab, there * 2 + core_at(step)),
            device_id_type=MESH,
        )

    for n in range(15):
        stat_copy(n).start()
    stat_in[place] = stat_out[...]
    for i in range(4):
        white_ref[:, pl.ds(i * 128, 128)] = jnp.transpose(
            wide_rows[pl.ds(i * 128, 128), :]
        ).astype(BF16)
    settle(stat_in.at[pl.ds(0, 15)], stat_recv)
    total = stat_in[0]
    for n in range(1, 16):
        total = total + stat_in[n]
    total_out[...] = total

    def total_copy(i):
        return pltpu.make_async_remote_copy(
            src_ref=total_out,
            dst_ref=total_in.at[slab],
            send_sem=total_send,
            recv_sem=total_recv,
            device_id=(slab_at(SLABS[i]), place),
            device_id_type=MESH,
        )

    for i in range(7):
        total_copy(i).start()
    total_in[slab] = total_out[...]

    settle(slab_in, slab_send)
    settle(moments.at[0, pl.ds(0, 15)], early_send)
    settle(moments.at[1, pl.ds(0, 15)], late_send)
    settle(wide_in.at[:, pl.ds(0, 15)], wide_send)
    settle(stat_in.at[pl.ds(0, 15)], stat_send)

    settle(total_in.at[pl.ds(0, 7)], total_send)
    settle(total_in.at[pl.ds(0, 7)], total_recv)
    total = total_in[0]
    for i in range(1, 8):
        total = total + total_in[i]
    stat_ref[...] = total


def finish(white_in, stat_in, white_ref, stat_ref):
    white_ref[...] = white_in[...]
    stat_ref[...] = stat_in[0:4] * (1.0 / LANDMARKS)


def local(embeddings, landmarks, factor, flips, labels, counts):
    any_space = pl.BlockSpec(memory_space=pl.ANY)
    vmem = pl.BlockSpec(memory_space=pltpu.VMEM)
    dma = pltpu.SemaphoreType.DMA
    whitened, statistic = pl.pallas_call(
        kernel,
        out_shape=(
            jax.ShapeDtypeStruct((128, 512), BF16),
            jax.ShapeDtypeStruct((8, 128), F32),
        ),
        in_specs=[pl.BlockSpec(memory_space=pltpu.SMEM), vmem] + [any_space] * 4,
        out_specs=(vmem, vmem),
        scratch_shapes=[
            pltpu.VMEM((ROWS, D), BF16),
            pltpu.VMEM((CHUNK * CHUNKS, D), BF16),
            pltpu.VMEM((2, ROWS, 2048), BF16),
            pltpu.VMEM((512, ROWS), jnp.int32),
            pltpu.VMEM((512, ROWS), BF16),
            pltpu.VMEM((ROWS, CHUNK), BF16),
            pltpu.VMEM((ROWS, 128), F32),
            pltpu.VMEM((ROWS, 128), F32),
            pltpu.VMEM((ROWS, 128), F32),
            pltpu.VMEM((ROWS, 128), F32),
            pltpu.VMEM((ROWS, CHUNK), F32),
            pltpu.VMEM((CHUNKS, 512, CHUNK), BF16),
            pltpu.VMEM((CHUNKS, 7, 64, CHUNK), BF16),
            pltpu.VMEM((2, 2, PART, ROWS), BF16),
            pltpu.VMEM((2, 16, PART, ROWS), BF16),
            pltpu.VMEM((2, 8, 2, 8 * PART, 128), BF16),
            pltpu.VMEM((2, 16, 8 * PART, 128), BF16),
            pltpu.VMEM((512, 128), F32),
            pltpu.VMEM((2, 8, 128), F32),
            pltpu.VMEM((7, 2, 8, 128), F32),
            pltpu.VMEM((8, 128), F32),
            pltpu.VMEM((16, 8, 128), F32),
            pltpu.VMEM((8, 128), F32),
            pltpu.VMEM((8, 8, 128), F32),
            dma((BLOCKS,)),
            dma((CHUNKS,)),
            dma,
            dma,
            dma,
            dma,
            dma,
            dma,
            dma,
            dma((CHUNKS,)),
            dma,
            dma,
            dma,
            dma,
            dma,
            dma((2,)),
            dma,
            dma,
            dma,
            dma,
        ],
        compiler_params=pltpu.CompilerParams(
            collective_id=0, has_side_effects=True, vmem_limit_bytes=60 << 20
        ),
    )(counts, labels.reshape(8, 128), embeddings, landmarks, factor, flips)
    whitened, statistic = pl.pallas_call(
        finish,
        out_shape=(
            jax.ShapeDtypeStruct((128, 512), BF16),
            jax.ShapeDtypeStruct((4, 128), F32),
        ),
        in_specs=[vmem, vmem],
        out_specs=(vmem, vmem),
    )(whitened, statistic)
    return whitened, statistic.reshape(512)


def solution(mesh):
    return jax.shard_map(
        local,
        mesh=mesh,
        in_specs=(
            P("sample", None),
            P("landmark", None),
            P("landmark", "sample"),
            P(None, "sample"),
            P("sample"),
            P(),
        ),
        out_specs=(P(("sample", "landmark"), None), P()),
        check_vma=False,
    )
```

time: 74.4 us -> 65.5 us (0.88)
  Pallas kernels: 70.7 us -> 64.7 us
  local copies, waits for them, and re-layouts: 2.83 us -> 0 us
    pallas_call x1, Pallas kernels: 70.7 us -> 63.1 us  [local(): pl.pallas_call(kernel, out_shape=(jax.ShapeDtypeStruct((128, 512), BF16),...]
    unnamed x2 -> x0, local copies, waits for them, and re-layouts: 2.83 us -> none
    pallas_call x0 -> x1, Pallas kernels: none -> 1.57 us  [local(): pl.pallas_call(finish, out_shape=(jax.ShapeDtypeStruct((128, 512), BF16),...]
where the time goes in v2:
time: 65.5 us; the launch traced here: 65.3 us
  Pallas kernels  64.7 us (99%)
    pallas_call x1, Pallas kernels, local(): pl.pallas_call(kernel, out_shape=(jax.ShapeDtypeStruct((128, 512), BF16),...  63.1 us
    pallas_call x1, Pallas kernels, local(): pl.pallas_call(finish, out_shape=(jax.ShapeDtypeStruct((128, 512), BF16),...  1.57 us

profile of v2, /device:TPU:1, one launch (start us, length us, event | category | flops | bytes accessed | tf_op | source)
XLA Modules:
  0.0 65.3 jit_solution(5066029975808676222)
XLA Ops:
  0.6 63.1 %shard_map.77 = (bf16[128,512]{1,0:T(8,128)(2,1)}, f32[8,128]{1,0:T(8,128)}) custom-call(s32[8]{0:T(128)} %counts_ref.1, s32[8,128]{1,0:T(8,128)} %bitcast.2, bf16[1024,4096]{1,0:T(8,128)(2,1)} %emb_hbm.1, bf16[1024,4096]{1,0:T(8,128)(2,1)} %land_hbm.1, bf16[1024,2048]{1,0:T(8,128)(2,1)} %factor_hbm.1, s32[512,1024]{1,0:T(8,128)} %flips_hbm.1), custom_call_target="tpu_custom_call" | custom-call | tf_op jit(solution)/shard_map/pallas_call | solution.py:411
  63.8 1.6 %shard_map.78 = (bf16[128,512]{1,0:T(8,128)(2,1)}, f32[4,128]{1,0:T(4,128)}) custom-call(bf16[128,512]{1,0:T(8,128)(2,1)} %get-tuple-element.6.white_in, f32[8,128]{1,0:T(8,128)} %get-tuple-element.7.stat_in), custom_call_target="tpu_custom_call" | custom-call | tf_op jit(solution)/shard_map/pallas_call | solution.py:469

commit v3 on v2

--- a/solution.py
+++ b/solution.py
@@ -16,20 +16,24 @@
 BLOCK = 256
 BLOCKS = ROWS // BLOCK
 PART = 16
+STEPS = [2, 1, 3, 0]
 
 SLABS = [(1, 2), (1, 1), (1, 3), (0, 2), (1, 0), (0, 1), (0, 3)]
 CHIPS = [(1, 2), (1, 1), (1, 3), (0, 2), (1, 0), (0, 1), (0, 3)]
+AROUND = [(a, b) for a in SLABS + [(0, 0)] for b in CHIPS + [(0, 0)]][:63]
 
 
 def kernel(
     counts_ref, labels_ref, emb_hbm, land_hbm, factor_hbm, flips_hbm,
     white_ref, stat_ref,
     emb, land, factor, flips, signs, weighted, row_scale, col_a, col_b, col_w, kern,
-    partial_buf, slab_in, own_sum, moments, wide_out, wide_in, wide_rows,
-    count_out, count_in, stat_out, stat_in, total_out, total_in,
+    partial_buf, slab_in, own_sum, moments, wide_out, wide_in,
+    line_out, line_in, line_own, hop_out, hop_in, wide_rows,
+    count_out, count_in, stat_out, stat_in, total_in,
     emb_sem, land_sem, factor_sem, flips_sem,
     factor_send, factor_recv, count_send, count_recv, slab_send, slab_recv,
-    early_send, early_recv, late_send, late_recv, wide_send, wide_recv, stat_send, stat_recv, total_send, total_recv,
+    early_send, early_recv, late_send, late_recv, wide_send, wide_recv,
+    line_send, line_recv, hop_send, hop_recv, stat_send, stat_recv, total_send, total_recv,
 ):
     slab = lax.axis_index("sample")
     place = lax.axis_index("landmark")
@@ -87,8 +91,10 @@
         for step in range(2):
             friends.append((slab_at(offset), here + core_at(step)))
     for offset in CHIPS:
-        for step in range(2):
-            friends.append((slab, chip_at(offset) * 2 + core_at(step)))
+        friends.append((slab, chip_at(offset) * 2 + other))
+    for offset in AROUND:
+        if offset[1] != (0, 0):
+            friends.append((slab_at(offset[0]), chip_at(offset[1]) * 2 + core))
     for friend in friends:
         pl.semaphore_signal(barrier, inc=1, device_id=friend, device_id_type=MESH)
 
@@ -193,26 +199,25 @@
     land_copy(0).wait()
     first_scale = point_scale(0)
 
-    def first_block(b, _):
-        start = pl.multiple_of(b * BLOCK, BLOCK)
-        emb_copy(b).wait()
-        for q in range(BLOCK // 64):
-            rows = pl.multiple_of(start + q * 64, 64)
+    def first_rows(start, count):
+        for b in range(start // BLOCK, (start + count) // BLOCK):
+            emb_copy(b).wait()
+        for q in range(count // 64):
+            rows = start + q * 64
             total = jnp.sum(squares(emb, rows, 64), axis=1, keepdims=True)
             row_scale[pl.ds(rows, 64), :] = jnp.broadcast_to(
                 lax.rsqrt(total * (1.0 / D) + 1e-6) * fold, (64, 128)
             )
         cross = lax.dot_general(
-            emb[pl.ds(start, BLOCK), :],
+            emb[pl.ds(start, count), :],
             land[0:CHUNK, :],
             (((1,), (1,)), ((), ())),
             preferred_element_type=F32,
         )
-        scale = wide2(row_scale[pl.ds(start, BLOCK), :])
-        kern[pl.ds(start, BLOCK), :] = jnp.exp2(cross * scale * first_scale)
-        return 0
-
-    first_block(0, 0)
+        scale = wide2(row_scale[pl.ds(start, count), :])
+        kern[pl.ds(start, count), :] = jnp.exp2(cross * scale * first_scale)
+
+    first_rows(0, BLOCK)
     pl.semaphore_wait(barrier, len(friends))
 
     def count_copy(i):
@@ -230,7 +235,8 @@
     flips_copy.start()
     for k in range(1, CHUNKS):
         land_copy(k).start()
-    lax.fori_loop(1, BLOCKS, first_block, 0)
+    first_rows(BLOCK, BLOCK)
+    first_rows(2 * BLOCK, 2 * BLOCK)
 
     eye = lax.broadcasted_iota(jnp.int32, (128, 128), 0) == lax.broadcasted_iota(
         jnp.int32, (128, 128), 1
@@ -291,110 +297,150 @@
     settle(factor.at[core], factor_send)
     settle(factor.at[other], factor_recv)
 
-    def wide_copy(h, t, step):
+    def wide_copy(t, step):
         chip = chip_at(CHIPS[t]) if t < 7 else y_lo * 4 + x
         return pltpu.make_async_remote_copy(
-            src_ref=wide_out.at[h, t, core_at(step)],
-            dst_ref=wide_in.at[h, core * 8 + t],
+            src_ref=wide_out.at[t, core_at(step)],
+            dst_ref=wide_in.at[core * 8 + t],
             send_sem=wide_send,
-            recv_sem=wide_recv.at[h],
+            recv_sem=wide_recv,
             device_id=(slab, chip * 2 + core_at(step)),
             device_id_type=MESH,
         )
 
-    def whiten(h):
-        left = jnp.concatenate(
+    def line_copy(t, step):
+        return pltpu.make_async_remote_copy(
+            src_ref=line_out.at[t, core_at(step)],
+            dst_ref=line_in.at[core * 4 + t],
+            send_sem=line_send,
+            recv_sem=line_recv,
+            device_id=(slab, (y_lo * 4 + (x + STEPS[t]) % 4) * 2 + core_at(step)),
+            device_id_type=MESH,
+        )
+
+    hop = pltpu.make_async_remote_copy(
+        src_ref=hop_out,
+        dst_ref=hop_in,
+        send_sem=hop_send,
+        recv_sem=hop_recv,
+        device_id=(slab, ((1 - y_lo) * 4 + x) * 2 + core),
+        device_id_type=MESH,
+    )
+
+    def left_of(h):
+        return jnp.concatenate(
             [moments[h, c * 8 : c * 8 + 8].reshape(8 * PART, ROWS) for c in range(2)], axis=1
         )
+
+    def tile(left, chip):
+        columns = pl.ds(pl.multiple_of(chip * 256, 256), 256)
+        return jnp.dot(
+            left,
+            jnp.concatenate([factor[0, :, columns], factor[1, :, columns]], axis=0),
+            preferred_element_type=F32,
+        ).astype(BF16)
+
+    def place_rows(h, c, total):
+        for s in range(8):
+            wide_rows[pl.ds(s * 64 + c * 32 + h * PART, PART), :] = total[
+                s * PART : (s + 1) * PART
+            ]
+
+    def early_whiten():
+        left = left_of(0)
+        for t in range(4):
+            for side in range(2):
+                value = tile(left, side * 4 + (x + STEPS[t]) % 4)
+                line_out[t, 0, side] = value[:, :128]
+                line_out[t, 1, side] = value[:, 128:]
+            if t < 3:
+                line_copy(t, 0).start()
+            line_copy(t, 1).start()
+        line_in[core * 4 + 3] = line_out[3, core]
+
+    def late_whiten():
+        left = left_of(1)
         for t in range(8):
-            q = chip_at(CHIPS[t]) if t < 7 else y_lo * 4 + x
-            columns = pl.ds(pl.multiple_of(q * 256, 256), 256)
-            value = jnp.dot(
-                left,
-                jnp.concatenate([factor[0, :, columns], factor[1, :, columns]], axis=0),
-                preferred_element_type=F32,
-            ).astype(BF16)
-            wide_out[h, t, 0] = value[:, :128]
-            wide_out[h, t, 1] = value[:, 128:]
+            value = tile(left, chip_at(CHIPS[t]) if t < 7 else y_lo * 4 + x)
+            wide_out[t, 0] = value[:, :128]
+            wide_out[t, 1] = value[:, 128:]
             if t < 7:
-                wide_copy(h, t, 0).start()
-            wide_copy(h, t, 1).start()
-        wide_in[h, core * 8 + 7] = wide_out[h, 7, core]
-
-    def gather(h):
-        settle(wide_in.at[h, pl.ds(0, 15)], wide_recv.at[h])
-        for c in range(2):
-            total = wide_in[h, c * 8].astype(F32)
-            for t in range(1, 8):
-                total = total + wide_in[h, c * 8 + t].astype(F32)
-            for s in range(8):
-                wide_rows[pl.ds(s * 64 + c * 32 + h * PART, PART), :] = total[
-                    s * PART : (s + 1) * PART
-                ]
+                wide_copy(t, 0).start()
+            wide_copy(t, 1).start()
+        wide_in[core * 8 + 7] = wide_out[7, core]
+
+    def line_sum(c, side):
+        total = line_in[c * 4, side].astype(F32)
+        for t in range(1, 4):
+            total = total + line_in[c * 4 + t, side].astype(F32)
+        return total
 
     settle(moments.at[0, pl.ds(0, 15)], early_recv)
-    whiten(0)
+    early_whiten()
     settle(moments.at[1, pl.ds(0, 15)], late_recv)
-    whiten(1)
-    gather(0)
-    gather(1)
+    late_whiten()
+    settle(line_in.at[pl.ds(0, 7)], line_recv)
+    for c in range(2):
+        hop_out[c] = line_sum(c, 1 - y_lo).astype(BF16)
+    hop.start()
+    for c in range(2):
+        line_own[c] = line_sum(c, y_lo)
+    hop.wait_recv()
+    for c in range(2):
+        place_rows(0, c, line_own[c] + hop_in[c].astype(F32))
+    settle(wide_in.at[pl.ds(0, 15)], wide_recv)
+    for c in range(2):
+        total = wide_in[c * 8].astype(F32)
+        for t in range(1, 8):
+            total = total + wide_in[c * 8 + t].astype(F32)
+        place_rows(1, c, total)
     values = wide_rows[...]
     norms = lane_sums(values * values)[0:1]
     for i in range(4):
         stat_out[pl.ds(i, 1), :] = norms[:, i * 128 : (i + 1) * 128]
     stat_out[pl.ds(4, 4), :] = jnp.zeros((4, 128), F32)
 
-    def stat_copy(n):
-        if n < 14:
-            there, step = chip_at(CHIPS[n // 2]), n % 2
-        else:
-            there, step = y_lo * 4 + x, 1
-        return pltpu.make_async_remote_copy(
-            src_ref=stat_out,
-            dst_ref=stat_in.at[place],
-            send_sem=stat_send,
-            recv_sem=stat_recv,
-            device_id=(slab, there * 2 + core_at(step)),
-            device_id_type=MESH,
-        )
-
-    for n in range(15):
-        stat_copy(n).start()
-    stat_in[place] = stat_out[...]
+    pair = pltpu.make_async_remote_copy(
+        src_ref=stat_out,
+        dst_ref=stat_in,
+        send_sem=stat_send,
+        recv_sem=stat_recv,
+        device_id=(slab, here + other),
+        device_id_type=MESH,
+    )
+    pair.start()
+    pair.wait()
+    total_in[slab * 8 + y_lo * 4 + x] = stat_out[...] + stat_in[...]
+
+    def total_copy(n):
+        slot = slab * 8 + y_lo * 4 + x
+        return pltpu.make_async_remote_copy(
+            src_ref=total_in.at[slot],
+            dst_ref=total_in.at[slot],
+            send_sem=total_send,
+            recv_sem=total_recv,
+            device_id=(slab_at(AROUND[n][0]), chip_at(AROUND[n][1]) * 2 + core),
+            device_id_type=MESH,
+        )
+
+    for n in range(63):
+        total_copy(n).start()
     for i in range(4):
         white_ref[:, pl.ds(i * 128, 128)] = jnp.transpose(
             wide_rows[pl.ds(i * 128, 128), :]
         ).astype(BF16)
-    settle(stat_in.at[pl.ds(0, 15)], stat_recv)
-    total = stat_in[0]
-    for n in range(1, 16):
-        total = total + stat_in[n]
-    total_out[...] = total
-
-    def total_copy(i):
-        return pltpu.make_async_remote_copy(
-            src_ref=total_out,
-            dst_ref=total_in.at[slab],
-            send_sem=total_send,
-            recv_sem=total_recv,
-            device_id=(slab_at(SLABS[i]), place),
-            device_id_type=MESH,
-        )
-
-    for i in range(7):
-        total_copy(i).start()
-    total_in[slab] = total_out[...]
 
     settle(slab_in, slab_send)
     settle(moments.at[0, pl.ds(0, 15)], early_send)
     settle(moments.at[1, pl.ds(0, 15)], late_send)
-    settle(wide_in.at[:, pl.ds(0, 15)], wide_send)
-    settle(stat_in.at[pl.ds(0, 15)], stat_send)
-
-    settle(total_in.at[pl.ds(0, 7)], total_send)
-    settle(total_in.at[pl.ds(0, 7)], total_recv)
+    settle(wide_in.at[pl.ds(0, 15)], wide_send)
+    settle(line_in.at[pl.ds(0, 7)], line_send)
+    hop.wait_send()
+
+    settle(total_in.at[pl.ds(0, 63)], total_send)
+    settle(total_in.at[pl.ds(0, 63)], total_recv)
     total = total_in[0]
-    for i in range(1, 8):
+    for i in range(1, 64):
         total = total + total_in[i]
     stat_ref[...] = total
 
@@ -432,15 +478,19 @@
             pltpu.VMEM((CHUNKS, 7, 64, CHUNK), BF16),
             pltpu.VMEM((2, 2, PART, ROWS), BF16),
             pltpu.VMEM((2, 16, PART, ROWS), BF16),
-            pltpu.VMEM((2, 8, 2, 8 * PART, 128), BF16),
-            pltpu.VMEM((2, 16, 8 * PART, 128), BF16),
+            pltpu.VMEM((8, 2, 8 * PART, 128), BF16),
+            pltpu.VMEM((16, 8 * PART, 128), BF16),
+            pltpu.VMEM((4, 2, 2, 8 * PART, 128), BF16),
+            pltpu.VMEM((8, 2, 8 * PART, 128), BF16),
+            pltpu.VMEM((2, 8 * PART, 128), F32),
+            pltpu.VMEM((2, 8 * PART, 128), BF16),
+            pltpu.VMEM((2, 8 * PART, 128), BF16),
             pltpu.VMEM((512, 128), F32),
             pltpu.VMEM((2, 8, 128), F32),
             pltpu.VMEM((7, 2, 8, 128), F32),
             pltpu.VMEM((8, 128), F32),
-            pltpu.VMEM((16, 8, 128), F32),
             pltpu.VMEM((8, 128), F32),
-            pltpu.VMEM((8, 8, 128), F32),
+            pltpu.VMEM((64, 8, 128), F32),
             dma((BLOCKS,)),
             dma((CHUNKS,)),
             dma,
@@ -456,7 +506,11 @@
             dma,
             dma,
             dma,
-            dma((2,)),
+            dma,
+            dma,
+            dma,
+            dma,
+            dma,
             dma,
             dma,
             dma,

time: 65.5 us -> 65.9 us (level)
  no operation moved by 1% of the time
where the time goes in v3:
time: 65.9 us; the launch traced here: 65.8 us
  Pallas kernels  65.1 us (99%)
    pallas_call x1, Pallas kernels, local(): pl.pallas_call(kernel, out_shape=(jax.ShapeDtypeStruct((128, 512), BF16),...  63.6 us
    pallas_call x1, Pallas kernels, local(): pl.pallas_call(finish, out_shape=(jax.ShapeDtypeStruct((128, 512), BF16),...  1.57 us

profile of v3, /device:TPU:1, one launch (start us, length us, event | category | flops | bytes accessed | tf_op | source)
XLA Modules:
  0.0 65.8 jit_solution(17734316603444510454)
XLA Ops:
  0.6 63.6 %shard_map.77 = (bf16[128,512]{1,0:T(8,128)(2,1)}, f32[8,128]{1,0:T(8,128)}) custom-call(s32[8]{0:T(128)} %counts_ref.1, s32[8,128]{1,0:T(8,128)} %bitcast.2, bf16[1024,4096]{1,0:T(8,128)(2,1)} %emb_hbm.1, bf16[1024,4096]{1,0:T(8,128)(2,1)} %land_hbm.1, bf16[1024,2048]{1,0:T(8,128)(2,1)} %factor_hbm.1, s32[512,1024]{1,0:T(8,128)} %flips_hbm.1), custom_call_target="tpu_custom_call" | custom-call | tf_op jit(solution)/shard_map/pallas_call | solution.py:457
  64.2 1.6 %shard_map.78 = (bf16[128,512]{1,0:T(8,128)(2,1)}, f32[4,128]{1,0:T(4,128)}) custom-call(bf16[128,512]{1,0:T(8,128)(2,1)} %get-tuple-element.6.white_in, f32[8,128]{1,0:T(8,128)} %get-tuple-element.7.stat_in), custom_call_target="tpu_custom_call" | custom-call | tf_op jit(solution)/shard_map/pallas_call | solution.py:523

commit v4 on v3

--- a/solution.py
+++ b/solution.py
@@ -18,9 +18,9 @@
 PART = 16
 STEPS = [2, 1, 3, 0]
 
-SLABS = [(1, 2), (1, 1), (1, 3), (0, 2), (1, 0), (0, 1), (0, 3)]
+SLABS = [(1, 2), (0, 1), (1, 3), (0, 3), (1, 1), (0, 2), (1, 0)]
 CHIPS = [(1, 2), (1, 1), (1, 3), (0, 2), (1, 0), (0, 1), (0, 3)]
-AROUND = [(a, b) for a in SLABS + [(0, 0)] for b in CHIPS + [(0, 0)]][:63]
+COLUMN = [(a, b) for a in SLABS + [(0, 0)] for b in (1, 0)][:15]
 
 
 def kernel(
@@ -84,6 +84,7 @@
     land_copy(0).start()
     for b in range(BLOCKS):
         emb_copy(b).start()
+    flips_copy.start()
 
     barrier = pltpu.get_barrier_semaphore()
     friends = [(slab, here + other)]
@@ -91,10 +92,11 @@
         for step in range(2):
             friends.append((slab_at(offset), here + core_at(step)))
     for offset in CHIPS:
-        friends.append((slab, chip_at(offset) * 2 + other))
-    for offset in AROUND:
-        if offset[1] != (0, 0):
-            friends.append((slab_at(offset[0]), chip_at(offset[1]) * 2 + core))
+        for step in range(2):
+            friends.append((slab, chip_at(offset) * 2 + core_at(step)))
+    for offset in COLUMN[:14]:
+        if offset[1] == 1:
+            friends.append((slab_at(offset[0]), chip_at((1, 0)) * 2 + core))
     for friend in friends:
         pl.semaphore_signal(barrier, inc=1, device_id=friend, device_id_type=MESH)
 
@@ -108,6 +110,15 @@
     count_out[0] = jnp.broadcast_to(jnp.sum(in_a, keepdims=True), (8, 128))
     count_out[1] = jnp.broadcast_to(jnp.sum(in_b, keepdims=True), (8, 128))
 
+    eye = lax.broadcasted_iota(jnp.int32, (128, 128), 0) == lax.broadcasted_iota(
+        jnp.int32, (128, 128), 1
+    )
+    for row, column in ((in_a, col_a), (in_b, col_b)):
+        for i in range(8):
+            spread = jnp.where(eye, jnp.broadcast_to(row[i : i + 1], (128, 128)), 0.0)
+            column[pl.ds(i * 128, 128), :] = jnp.dot(
+                spread.astype(BF16), jnp.ones((128, 128), BF16), preferred_element_type=F32
+            )
     def squares(ref, start, count):
         total = jnp.zeros((count, 128), F32)
         for t in range(D // 128):
@@ -156,7 +167,7 @@
 
     def mom_target(n):
         if n < 14:
-            return slab_at(SLABS[n // 2]), n % 2
+            return slab_at(SLABS[n % 7]), n // 7
         return slab, 1
 
     def early_copy(k, n):
@@ -200,8 +211,6 @@
     first_scale = point_scale(0)
 
     def first_rows(start, count):
-        for b in range(start // BLOCK, (start + count) // BLOCK):
-            emb_copy(b).wait()
         for q in range(count // 64):
             rows = start + q * 64
             total = jnp.sum(squares(emb, rows, 64), axis=1, keepdims=True)
@@ -217,6 +226,7 @@
         scale = wide2(row_scale[pl.ds(start, count), :])
         kern[pl.ds(start, count), :] = jnp.exp2(cross * scale * first_scale)
 
+    emb_copy(0).wait()
     first_rows(0, BLOCK)
     pl.semaphore_wait(barrier, len(friends))
 
@@ -232,23 +242,17 @@
 
     for i in range(7):
         count_copy(i).start()
-    flips_copy.start()
-    for k in range(1, CHUNKS):
+    land_copy(1).start()
+    emb_copy(1).wait()
+    first_rows(BLOCK, BLOCK)
+    emb_copy(2).wait()
+    emb_copy(3).wait()
+    first_rows(2 * BLOCK, 2 * BLOCK)
+    for k in range(2, CHUNKS):
         land_copy(k).start()
-    first_rows(BLOCK, BLOCK)
-    first_rows(2 * BLOCK, 2 * BLOCK)
-
-    eye = lax.broadcasted_iota(jnp.int32, (128, 128), 0) == lax.broadcasted_iota(
-        jnp.int32, (128, 128), 1
-    )
-    for row, column in ((in_a, col_a), (in_b, col_b)):
-        for i in range(8):
-            spread = jnp.where(eye, jnp.broadcast_to(row[i : i + 1], (128, 128)), 0.0)
-            column[pl.ds(i * 128, 128), :] = jnp.dot(
-                spread.astype(BF16), jnp.ones((128, 128), BF16), preferred_element_type=F32
-            )
     flips_copy.wait()
     signs[...] = (2 * flips[...] - 1).astype(F32).astype(BF16)
+
     settle(count_in, count_send)
     settle(count_in, count_recv)
     count_a, count_b = count_out[0], count_out[1]
@@ -279,16 +283,12 @@
         ).astype(BF16)
         send_moments(k)
 
-        @pl.when(k >= 2)
-        def _():
-            sum_slabs(k - 2)
-
         return 0
 
     lax.fori_loop(1, CHUNKS, later_chunk, 0)
 
-    sum_slabs(CHUNKS - 2)
-    sum_slabs(CHUNKS - 1)
+    for k in range(CHUNKS):
+        sum_slabs(k)
     for n in range(15):
         late_copy(n).start()
     for h in range(2):
@@ -400,30 +400,39 @@
         stat_out[pl.ds(i, 1), :] = norms[:, i * 128 : (i + 1) * 128]
     stat_out[pl.ds(4, 4), :] = jnp.zeros((4, 128), F32)
 
-    pair = pltpu.make_async_remote_copy(
-        src_ref=stat_out,
-        dst_ref=stat_in,
-        send_sem=stat_send,
-        recv_sem=stat_recv,
-        device_id=(slab, here + other),
-        device_id_type=MESH,
-    )
-    pair.start()
-    pair.wait()
-    total_in[slab * 8 + y_lo * 4 + x] = stat_out[...] + stat_in[...]
+    def stat_copy(n):
+        step, turn = (n // 2, n % 2) if n < 6 else (3, 1)
+        return pltpu.make_async_remote_copy(
+            src_ref=stat_out,
+            dst_ref=stat_in.at[x * 2 + core],
+            send_sem=stat_send,
+            recv_sem=stat_recv,
+            device_id=(slab, (y_lo * 4 + (x + STEPS[step]) % 4) * 2 + core_at(turn)),
+            device_id_type=MESH,
+        )
+
+    for n in range(7):
+        stat_copy(n).start()
+    stat_in[x * 2 + core] = stat_out[...]
+    settle(stat_in.at[pl.ds(0, 7)], stat_recv)
+    total = stat_in[0]
+    for n in range(1, 8):
+        total = total + stat_in[n]
+    slot = slab * 2 + y_lo
+    total_in[slot] = total
 
     def total_copy(n):
-        slot = slab * 8 + y_lo * 4 + x
+        offset, side = COLUMN[n]
         return pltpu.make_async_remote_copy(
             src_ref=total_in.at[slot],
             dst_ref=total_in.at[slot],
             send_sem=total_send,
             recv_sem=total_recv,
-            device_id=(slab_at(AROUND[n][0]), chip_at(AROUND[n][1]) * 2 + core),
-            device_id_type=MESH,
-        )
-
-    for n in range(63):
+            device_id=(slab_at(offset), chip_at((side, 0)) * 2 + core),
+            device_id_type=MESH,
+        )
+
+    for n in range(15):
         total_copy(n).start()
     for i in range(4):
         white_ref[:, pl.ds(i * 128, 128)] = jnp.transpose(
@@ -437,10 +446,11 @@
     settle(line_in.at[pl.ds(0, 7)], line_send)
     hop.wait_send()
 
-    settle(total_in.at[pl.ds(0, 63)], total_send)
-    settle(total_in.at[pl.ds(0, 63)], total_recv)
+    settle(stat_in.at[pl.ds(0, 7)], stat_send)
+    settle(total_in.at[pl.ds(0, 15)], total_send)
+    settle(total_in.at[pl.ds(0, 15)], total_recv)
     total = total_in[0]
-    for i in range(1, 64):
+    for i in range(1, 16):
         total = total + total_in[i]
     stat_ref[...] = total
 
@@ -489,8 +499,8 @@
             pltpu.VMEM((2, 8, 128), F32),
             pltpu.VMEM((7, 2, 8, 128), F32),
             pltpu.VMEM((8, 128), F32),
-            pltpu.VMEM((8, 128), F32),
-            pltpu.VMEM((64, 8, 128), F32),
+            pltpu.VMEM((8, 8, 128), F32),
+            pltpu.VMEM((16, 8, 128), F32),
             dma((BLOCKS,)),
             dma((CHUNKS,)),
             dma,

time: 65.9 us -> 66.9 us (1.015)
  Pallas kernels: 65.1 us -> 66.1 us
    pallas_call x1, Pallas kernels: 63.6 us -> 64.5 us  [local(): pl.pallas_call(kernel, out_shape=(jax.ShapeDtypeStruct((128, 512), BF16),...]
where the time goes in v4:
time: 66.9 us; the launch traced here: 66.7 us
  Pallas kernels  66.1 us (99%)
    pallas_call x1, Pallas kernels, local(): pl.pallas_call(kernel, out_shape=(jax.ShapeDtypeStruct((128, 512), BF16),...  64.5 us
    pallas_call x1, Pallas kernels, local(): pl.pallas_call(finish, out_shape=(jax.ShapeDtypeStruct((128, 512), BF16),...  1.57 us

profile of v4, /device:TPU:1, one launch (start us, length us, event | category | flops | bytes accessed | tf_op | source)
XLA Modules:
  0.0 66.7 jit_solution(6202056226261811854)
XLA Ops:
  0.6 64.5 %shard_map.77 = (bf16[128,512]{1,0:T(8,128)(2,1)}, f32[8,128]{1,0:T(8,128)}) custom-call(s32[8]{0:T(128)} %counts_ref.1, s32[8,128]{1,0:T(8,128)} %bitcast.2, bf16[1024,4096]{1,0:T(8,128)(2,1)} %emb_hbm.1, bf16[1024,4096]{1,0:T(8,128)(2,1)} %land_hbm.1, bf16[1024,2048]{1,0:T(8,128)(2,1)} %factor_hbm.1, s32[512,1024]{1,0:T(8,128)} %flips_hbm.1), custom_call_target="tpu_custom_call" | custom-call | tf_op jit(solution)/shard_map/pallas_call | solution.py:467
  65.2 1.6 %shard_map.78 = (bf16[128,512]{1,0:T(8,128)(2,1)}, f32[4,128]{1,0:T(4,128)}) custom-call(bf16[128,512]{1,0:T(8,128)(2,1)} %get-tuple-element.6.white_in, f32[8,128]{1,0:T(8,128)} %get-tuple-element.7.stat_in), custom_call_target="tpu_custom_call" | custom-call | tf_op jit(solution)/shard_map/pallas_call | solution.py:533

commit v5 on v2

--- a/solution.py
+++ b/solution.py
@@ -19,6 +19,8 @@
 
 SLABS = [(1, 2), (1, 1), (1, 3), (0, 2), (1, 0), (0, 1), (0, 3)]
 CHIPS = [(1, 2), (1, 1), (1, 3), (0, 2), (1, 0), (0, 1), (0, 3)]
+COLUMN = [(a, b) for a in SLABS + [(0, 0)] for b in (1, 0)][:15]
+STEPS = [2, 1, 3, 0]
 
 
 def kernel(
@@ -26,7 +28,7 @@
     white_ref, stat_ref,
     emb, land, factor, flips, signs, weighted, row_scale, col_a, col_b, col_w, kern,
     partial_buf, slab_in, own_sum, moments, wide_out, wide_in, wide_rows,
-    count_out, count_in, stat_out, stat_in, total_out, total_in,
+    count_out, count_in, stat_out, stat_in, total_in,
     emb_sem, land_sem, factor_sem, flips_sem,
     factor_send, factor_recv, count_send, count_recv, slab_send, slab_recv,
     early_send, early_recv, late_send, late_recv, wide_send, wide_recv, stat_send, stat_recv, total_send, total_recv,
@@ -89,6 +91,9 @@
     for offset in CHIPS:
         for step in range(2):
             friends.append((slab, chip_at(offset) * 2 + core_at(step)))
+    for offset in COLUMN[:14]:
+        if offset[1] == 1:
+            friends.append((slab_at(offset[0]), chip_at((1, 0)) * 2 + core))
     for friend in friends:
         pl.semaphore_signal(barrier, inc=1, device_id=friend, device_id_type=MESH)
 
@@ -102,6 +107,15 @@
     count_out[0] = jnp.broadcast_to(jnp.sum(in_a, keepdims=True), (8, 128))
     count_out[1] = jnp.broadcast_to(jnp.sum(in_b, keepdims=True), (8, 128))
 
+    eye = lax.broadcasted_iota(jnp.int32, (128, 128), 0) == lax.broadcasted_iota(
+        jnp.int32, (128, 128), 1
+    )
+    for row, column in ((in_a, col_a), (in_b, col_b)):
+        for i in range(8):
+            spread = jnp.where(eye, jnp.broadcast_to(row[i : i + 1], (128, 128)), 0.0)
+            column[pl.ds(i * 128, 128), :] = jnp.dot(
+                spread.astype(BF16), jnp.ones((128, 128), BF16), preferred_element_type=F32
+            )
     def squares(ref, start, count):
         total = jnp.zeros((count, 128), F32)
         for t in range(D // 128):
@@ -193,26 +207,25 @@
     land_copy(0).wait()
     first_scale = point_scale(0)
 
-    def first_block(b, _):
-        start = pl.multiple_of(b * BLOCK, BLOCK)
-        emb_copy(b).wait()
-        for q in range(BLOCK // 64):
-            rows = pl.multiple_of(start + q * 64, 64)
+    def first_rows(start, count):
+        for b in range(start // BLOCK, (start + count) // BLOCK):
+            emb_copy(b).wait()
+        for q in range(count // 64):
+            rows = start + q * 64
             total = jnp.sum(squares(emb, rows, 64), axis=1, keepdims=True)
             row_scale[pl.ds(rows, 64), :] = jnp.broadcast_to(
                 lax.rsqrt(total * (1.0 / D) + 1e-6) * fold, (64, 128)
             )
         cross = lax.dot_general(
-            emb[pl.ds(start, BLOCK), :],
+            emb[pl.ds(start, count), :],
             land[0:CHUNK, :],
             (((1,), (1,)), ((), ())),
             preferred_element_type=F32,
         )
-        scale = wide2(row_scale[pl.ds(start, BLOCK), :])
-        kern[pl.ds(start, BLOCK), :] = jnp.exp2(cross * scale * first_scale)
-        return 0
-
-    first_block(0, 0)
+        scale = wide2(row_scale[pl.ds(start, count), :])
+        kern[pl.ds(start, count), :] = jnp.exp2(cross * scale * first_scale)
+
+    first_rows(0, BLOCK)
     pl.semaphore_wait(barrier, len(friends))
 
     def count_copy(i):
@@ -230,17 +243,9 @@
     flips_copy.start()
     for k in range(1, CHUNKS):
         land_copy(k).start()
-    lax.fori_loop(1, BLOCKS, first_block, 0)
-
-    eye = lax.broadcasted_iota(jnp.int32, (128, 128), 0) == lax.broadcasted_iota(
-        jnp.int32, (128, 128), 1
-    )
-    for row, column in ((in_a, col_a), (in_b, col_b)):
-        for i in range(8):
-            spread = jnp.where(eye, jnp.broadcast_to(row[i : i + 1], (128, 128)), 0.0)
-            column[pl.ds(i * 128, 128), :] = jnp.dot(
-                spread.astype(BF16), jnp.ones((128, 128), BF16), preferred_element_type=F32
-            )
+    first_rows(BLOCK, BLOCK)
+    first_rows(2 * BLOCK, 2 * BLOCK)
+
     flips_copy.wait()
     signs[...] = (2 * flips[...] - 1).astype(F32).astype(BF16)
     settle(count_in, count_send)
@@ -345,56 +350,54 @@
     stat_out[pl.ds(4, 4), :] = jnp.zeros((4, 128), F32)
 
     def stat_copy(n):
-        if n < 14:
-            there, step = chip_at(CHIPS[n // 2]), n % 2
-        else:
-            there, step = y_lo * 4 + x, 1
+        step, turn = (n // 2, n % 2) if n < 6 else (3, 1)
         return pltpu.make_async_remote_copy(
             src_ref=stat_out,
-            dst_ref=stat_in.at[place],
+            dst_ref=stat_in.at[x * 2 + core],
             send_sem=stat_send,
             recv_sem=stat_recv,
-            device_id=(slab, there * 2 + core_at(step)),
+            device_id=(slab, (y_lo * 4 + (x + STEPS[step]) % 4) * 2 + core_at(turn)),
+            device_id_type=MESH,
+        )
+
+    for n in range(7):
+        stat_copy(n).start()
+    stat_in[x * 2 + core] = stat_out[...]
+    settle(stat_in.at[pl.ds(0, 7)], stat_recv)
+    total = stat_in[0]
+    for n in range(1, 8):
+        total = total + stat_in[n]
+    slot = slab * 2 + y_lo
+    total_in[slot] = total
+
+    def total_copy(n):
+        offset, side = COLUMN[n]
+        return pltpu.make_async_remote_copy(
+            src_ref=total_in.at[slot],
+            dst_ref=total_in.at[slot],
+            send_sem=total_send,
+            recv_sem=total_recv,
+            device_id=(slab_at(offset), chip_at((side, 0)) * 2 + core),
             device_id_type=MESH,
         )
 
     for n in range(15):
-        stat_copy(n).start()
-    stat_in[place] = stat_out[...]
+        total_copy(n).start()
     for i in range(4):
         white_ref[:, pl.ds(i * 128, 128)] = jnp.transpose(
             wide_rows[pl.ds(i * 128, 128), :]
         ).astype(BF16)
-    settle(stat_in.at[pl.ds(0, 15)], stat_recv)
-    total = stat_in[0]
-    for n in range(1, 16):
-        total = total + stat_in[n]
-    total_out[...] = total
-
-    def total_copy(i):
-        return pltpu.make_async_remote_copy(
-            src_ref=total_out,
-            dst_ref=total_in.at[slab],
-            send_sem=total_send,
-            recv_sem=total_recv,
-            device_id=(slab_at(SLABS[i]), place),
-            device_id_type=MESH,
-        )
-
-    for i in range(7):
-        total_copy(i).start()
-    total_in[slab] = total_out[...]
 
     settle(slab_in, slab_send)
     settle(moments.at[0, pl.ds(0, 15)], early_send)
     settle(moments.at[1, pl.ds(0, 15)], late_send)
     settle(wide_in.at[:, pl.ds(0, 15)], wide_send)
-    settle(stat_in.at[pl.ds(0, 15)], stat_send)
-
-    settle(total_in.at[pl.ds(0, 7)], total_send)
-    settle(total_in.at[pl.ds(0, 7)], total_recv)
+    settle(stat_in.at[pl.ds(0, 7)], stat_send)
+
+    settle(total_in.at[pl.ds(0, 15)], total_send)
+    settle(total_in.at[pl.ds(0, 15)], total_recv)
     total = total_in[0]
-    for i in range(1, 8):
+    for i in range(1, 16):
         total = total + total_in[i]
     stat_ref[...] = total
 
@@ -438,9 +441,8 @@
             pltpu.VMEM((2, 8, 128), F32),
             pltpu.VMEM((7, 2, 8, 128), F32),
             pltpu.VMEM((8, 128), F32),
+            pltpu.VMEM((8, 8, 128), F32),
             pltpu.VMEM((16, 8, 128), F32),
-            pltpu.VMEM((8, 128), F32),
-            pltpu.VMEM((8, 8, 128), F32),
             dma((BLOCKS,)),
             dma((CHUNKS,)),
             dma,

time: 65.5 us -> 67.6 us (1.032)
  Pallas kernels: 64.7 us -> 66.8 us
    pallas_call x1, Pallas kernels: 63.1 us -> 65.3 us  [local(): pl.pallas_call(kernel, out_shape=(jax.ShapeDtypeStruct((128, 512), BF16),...]
where the time goes in v5:
time: 67.6 us; the launch traced here: 67.5 us
  Pallas kernels  66.8 us (99%)
    pallas_call x1, Pallas kernels, local(): pl.pallas_call(kernel, out_shape=(jax.ShapeDtypeStruct((128, 512), BF16),...  65.3 us
    pallas_call x1, Pallas kernels, local(): pl.pallas_call(finish, out_shape=(jax.ShapeDtypeStruct((128, 512), BF16),...  1.57 us

profile of v5, /device:TPU:1, one launch (start us, length us, event | category | flops | bytes accessed | tf_op | source)
XLA Modules:
  0.0 67.5 jit_solution(13425220264961821870)
XLA Ops:
  0.6 65.3 %shard_map.77 = (bf16[128,512]{1,0:T(8,128)(2,1)}, f32[8,128]{1,0:T(8,128)}) custom-call(s32[8]{0:T(128)} %counts_ref.1, s32[8,128]{1,0:T(8,128)} %bitcast.2, bf16[1024,4096]{1,0:T(8,128)(2,1)} %emb_hbm.1, bf16[1024,4096]{1,0:T(8,128)(2,1)} %land_hbm.1, bf16[1024,2048]{1,0:T(8,128)(2,1)} %factor_hbm.1, s32[512,1024]{1,0:T(8,128)} %flips_hbm.1), custom_call_target="tpu_custom_call" | custom-call | tf_op jit(solution)/shard_map/pallas_call | solution.py:414
  65.9 1.6 %shard_map.78 = (bf16[128,512]{1,0:T(8,128)(2,1)}, f32[4,128]{1,0:T(4,128)}) custom-call(bf16[128,512]{1,0:T(8,128)(2,1)} %get-tuple-element.6.white_in, f32[8,128]{1,0:T(8,128)} %get-tuple-element.7.stat_in), custom_call_target="tpu_custom_call" | custom-call | tf_op jit(solution)/shard_map/pallas_call | solution.py:471
